TPU v7x, 32 devices: a whole 2x2x4 slice. The times are simulated.
32 devices in a mesh: gx: 4 (over x, core), gy: 8 (over z, y).
Axes of the slice: x: 2, y: 2, z: 4, core: 2. Of those that a mesh axis runs over, the one named last changes fastest.
Arguments:
- fine_source: bfloat16 [4, 8, 4, 8000], P('gx', 'gy'), may hold values from -6 to 6
- fine_blocks: bfloat16 [3, 12, 20, 20], replicated, may hold values from -0.5 to 0.5
- coarse_blocks: bfloat16 [3, 12, 20, 20], replicated, may hold values from -0.5 to 0.5
- child_filter_matrices: bfloat16 [2, 20, 20], replicated, may hold values from -1 to 1
Outputs:
- fine_result: float32 [4, 8, 4, 8000], P('gx', 'gy')
All inputs are finite; a program needn't handle non-finite values.
Results may differ from a plain program's by a relative error of at most 0.013.
Values may be sent and summed in bfloat16 or wider, within the bound.
A program may use at most 64 MiB of HBM per device.

v0:
```python
import jax
import jax.numpy as jnp
import numpy as np
from jax import lax
from jax.experimental import pallas as pl
from jax.experimental.pallas import tpu as pltpu
from jax.sharding import PartitionSpec as P

BF = jnp.bfloat16
F32 = jnp.float32
PAIR = 2
SUB = 32
LANES = 128


def shifted(block, axis, distance):
    devices = range(lax.axis_size(axis))
    route = [(i - distance, i) for i in devices if i - distance in devices]
    return lax.ppermute(block, axis, route)


def partner(block, axis):
    count = lax.axis_size(axis)
    return lax.ppermute(block, axis, [(i, i ^ 1) for i in range(count)])


SEL_X = np.zeros((4, 5, 3), np.float32)
SEL_X[0, 0, 1] = SEL_X[0, 1, 2] = SEL_X[0, 2, 0] = 1
SEL_X[1, 3, 1] = SEL_X[2, 4, 1] = SEL_X[3, 0, 1] = 1
SEL_Y = np.zeros((2, 4, 3), np.float32)
SEL_Y[0, 0, 1] = SEL_Y[0, 1, 2] = SEL_Y[0, 2, 0] = SEL_Y[1, 3, 1] = 1


def level_mats(blocks, boxes):
    _, terms, n, _ = blocks.shape
    groups = terms // PAIR
    sel_z = np.zeros((2, boxes, boxes, 3), np.float32)
    for z in range(boxes):
        sel_z[0, z, z, 1] = 1
        if z > 0:
            sel_z[1, z, z - 1, 2] = 1
        if z < boxes - 1:
            sel_z[1, z, z + 1, 0] = 1
    first = jnp.einsum("tde,emli->mtldi", jnp.asarray(SEL_X, BF), blocks)
    first = jnp.pad(first, ((0, 0), (0, 0), (0, 24 - n), (0, 0), (0, SUB - n)))
    first = first.reshape(groups, PAIR * 4 * 24, 5 * SUB)
    grouped = blocks.reshape(3, groups, PAIR, n, n)
    second = jnp.einsum(
        "qte,mf,egmlj->gmqlftj", jnp.asarray(SEL_Y, BF), jnp.eye(PAIR, dtype=BF), grouped
    )
    second = jnp.pad(second, ((0, 0),) * 3 + ((0, SUB - n),) + ((0, 0),) * 3)
    second = second.reshape(groups, PAIR * 2 * SUB, PAIR * 4 * n)
    third = jnp.einsum("qzwe,emlk->mqzkwl", jnp.asarray(sel_z, BF), blocks)
    third = third.reshape(terms * 2, boxes * n, boxes * n)
    third = jnp.pad(third, ((0, 0), (0, LANES - boxes * n), (0, LANES - boxes * n)))
    return first, second, third.reshape(terms * 2 * LANES, LANES)


def dot(a, b):
    return jnp.dot(a, b, preferred_element_type=F32)


def level(u, first, second, third, flip, mid, n):
    groups = first.shape[0]
    for g in range(groups):
        slot = flip.at[g % 2]
        width = PAIR * 4 * n
        for j in range(0, n, 2):
            a = dot(first[g], jnp.concatenate([u(j), u(j + 1)], axis=1))
            for h in range(2):
                for t in range(PAIR * 4):
                    slot[pl.ds(t * n + j + h, n, stride=width), :] = a[
                        t * 24 : t * 24 + n, h * LANES : (h + 1) * LANES
                    ]
        for l in range(0, n, 2):
            rhs = jnp.concatenate(
                [slot[l * width : (l + 1) * width, :], slot[(l + 1) * width : (l + 2) * width, :]],
                axis=1,
            ).astype(BF)
            b = dot(second[g], rhs).astype(BF)
            for h in range(2):
                for q in range(PAIR * 2):
                    at = (g * PAIR * 2 + q) * LANES
                    mid[(l + h) * SUB : (l + h + 1) * SUB, at : at + LANES] = b[
                        q * SUB : (q + 1) * SUB, h * LANES : (h + 1) * LANES
                    ]
    return dot(mid[...], third[...])


def single(u, first, second, third, slot, mid, n):
    for j in range(0, n, 2):
        a = dot(first[...], jnp.concatenate([u(j), u(j + 1)], axis=1))
        for h in range(2):
            slot[pl.ds(j + h, n, stride=SUB), :] = a[:n, h * LANES : (h + 1) * LANES]
    for l in range(0, n, 2):
        rhs = jnp.concatenate(
            [slot[l * SUB : l * SUB + n, :], slot[(l + 1) * SUB : (l + 1) * SUB + n, :]], axis=1
        ).astype(BF)
        b = dot(second[...], rhs).astype(BF)
        for h in range(2):
            mid[(l + h) * SUB : (l + h + 1) * SUB, :LANES] = b[:, h * LANES : (h + 1) * LANES]
    return dot(mid[:, :LANES], third[...])


def filter_kernel(u_ref, fx, fy, fz, out, flip, mid):
    n = u_ref.shape[0]
    s = single(lambda j: u_ref[j], fx, fy, fz, flip.at[0], mid, n)
    out[...] = s.reshape(n, SUB, LANES).astype(out.dtype)


def fine_kernel(u_ref, first, second, third, out, flip, mid):
    n = u_ref.shape[0]
    out[...] = level(lambda j: u_ref[j], first, second, third, flip, mid, n).reshape(out.shape)


def coarse_kernel(u_ref, first, second, third, ex, ey, ez, fine, out, flip, mid, res):
    n = u_ref.shape[0]
    s = level(lambda j: u_ref[j], first, second, third, flip, mid, n)
    res[...] = s.reshape(n, SUB, LANES).astype(BF)
    s = single(lambda j: res[j], ex, ey, ez, flip.at[0], mid, n)
    out[...] = fine[...] + s.reshape(out.shape)


def scratch(n, terms):
    return [
        pltpu.VMEM((2, n * PAIR * 4 * n, LANES), F32),
        pltpu.VMEM((n * SUB, terms * 2 * LANES), BF),
    ]


PARAMS = pltpu.CompilerParams(vmem_limit_bytes=60 * 1024 * 1024)


def padded_to(m, rows, cols):
    return jnp.pad(m, ((0, rows - m.shape[0]), (0, cols - m.shape[1])))


def shards(fine_source, fine_blocks, coarse_blocks, filters):
    boxes = fine_source.shape[2]
    parents = boxes // 2
    terms, n = fine_blocks.shape[1], fine_blocks.shape[2]
    raw = fine_source.reshape(boxes, n, n, n)
    own = raw.transpose(2, 1, 0, 3).reshape(n, n, boxes * n)
    own = jnp.pad(own, ((0, 0), (0, SUB - n), (0, LANES - boxes * n)))
    parity_x = lax.axis_index("gx") % 2
    parity_y = lax.axis_index("gy") % 2
    sx = lax.dynamic_index_in_dim(filters, parity_x, 0, keepdims=False)
    sy = lax.dynamic_index_in_dim(filters, parity_y, 0, keepdims=False)
    eye = jnp.eye(parents, dtype=BF)
    fz = jnp.einsum("po,ckn->pcnok", eye, filters).reshape(boxes * n, parents * n)
    ez = jnp.einsum("po,ckn->okpcn", eye, filters).reshape(parents * n, boxes * n)
    fz, ez = padded_to(fz, LANES, LANES), padded_to(ez, LANES, LANES)
    ex, ey = padded_to(sx.T, SUB, SUB), padded_to(sy.T, SUB, n)
    fx, fy = padded_to(sx, SUB, SUB), padded_to(sy, SUB, n)

    grid_out = jax.ShapeDtypeStruct((n, SUB, LANES), BF)
    partial = pl.pallas_call(
        filter_kernel, out_shape=grid_out, scratch_shapes=scratch(n, terms), compiler_params=PARAMS
    )(own, fx, fy, fz)
    sides = [shifted(own, "gx", -1), shifted(own, "gx", 1)]
    sides += [shifted(own, "gy", -1), shifted(own, "gy", 1)]
    fine_u = jnp.concatenate([own] + sides, axis=1)
    half = partial.astype(F32) + partner(partial, "gx").astype(F32)
    parent = (half + partner(half.astype(BF), "gy").astype(F32)).astype(BF)
    near = [shifted(parent, "gy", -2), shifted(parent, "gy", 2)]
    near += [shifted(parent, "gx", -2), shifted(parent, "gx", 2)]
    coarse_u = jnp.concatenate([parent] + near, axis=1)
    fine = pl.pallas_call(
        fine_kernel,
        out_shape=jax.ShapeDtypeStruct((n, SUB, LANES), F32),
        scratch_shapes=scratch(n, terms),
        compiler_params=PARAMS,
        cost_estimate=pl.CostEstimate(flops=4_000_000_000, bytes_accessed=4_000_000, transcendentals=0),
    )(fine_u, *level_mats(fine_blocks, boxes))
    out = pl.pallas_call(
        coarse_kernel,
        out_shape=jax.ShapeDtypeStruct((n, SUB, LANES), F32),
        scratch_shapes=scratch(n, terms) + [pltpu.VMEM((n, SUB, LANES), BF)],
        compiler_params=PARAMS,
    )(coarse_u, *level_mats(coarse_blocks, parents), ex, ey, ez, fine)
    out = out[:, :n, : boxes * n].reshape(n, n, boxes, n).transpose(2, 0, 1, 3)
    return out.reshape(1, 1, boxes, n * n * n)


def solution(mesh):
    in_specs = (P("gx", "gy", None, None), P(), P(), P())
    out_specs = P("gx", "gy", None, None)
    return jax.shard_map(shards, mesh=mesh, in_specs=in_specs, out_specs=out_specs, check_vma=False)
```

profile of v0, /device:TPU:0, one launch (start us, length us, event | category | flops | bytes accessed | tf_op | source)
XLA Modules:
  0.0 111.9 jit_solution(13191914033684972734)
XLA Ops:
  0.0 1.3 %reshape.48 = bf16[4,20,20,20]{3,2,1,0:T(8,128)(2,1)S(1)} reshape(bf16[1,1,4,8000]{3,2,1,0:T(4,128)(2,1)} %param.10) | data formatting | bytes 128000 | tf_op jit(solution)/shard_map/reshape | solution.py:142
  1.9 0.8 constant_dynamic-update-slice_fusion.9
  2.6 1.3 %collective-permute-start.6 = (bf16[20,32,128]{2,1,0:T(8,128)(2,1)}, bf16[20,32,128]{2,1,0:T(8,128)(2,1)}, u32[]{:S(2)}, u32[]{:S(2)}) collective-permute-start(bf16[20,32,128]{2,1,0:T(8,128)(2,1)} %get-tuple-element.8.u_ref), channel_id=1, source_target_pairs={{8,0},{16,8},{24,16},{9,1},{17,9},{25,17},{10,2},{18,10},{26,18},{... | collective-permute-start | bytes 491528 | tf_op jit(solution)/shard_map/ppermute | solution.py:19
  3.9 3.7 %collective-permute-start.7 = (bf16[20,32,128]{2,1,0:T(8,128)(2,1)}, bf16[20,32,128]{2,1,0:T(8,128)(2,1)}, u32[]{:S(2)}, u32[]{:S(2)}) collective-permute-start(bf16[20,32,128]{2,1,0:T(8,128)(2,1)} %get-tuple-element.8.u_ref), channel_id=1, source_target_pairs={{0,8},{8,16},{16,24},{1,9},{9,17},{17,25},{2,10},{10,18},{18,26},{... | collective-permute-start | bytes 491528 | tf_op jit(solution)/shard_map/ppermute | solution.py:19
  7.6 1.3 %collective-permute-start.8 = (bf16[20,32,128]{2,1,0:T(8,128)(2,1)}, bf16[20,32,128]{2,1,0:T(8,128)(2,1)}, u32[]{:S(2)}, u32[]{:S(2)}) collective-permute-start(bf16[20,32,128]{2,1,0:T(8,128)(2,1)} %get-tuple-element.8.u_ref), channel_id=1, source_target_pairs={{1,0},{2,1},{3,2},{4,3},{5,4},{6,5},{7,6},{9,8},{10,9},{11,10},{12... | collective-permute-start | bytes 491528 | tf_op jit(solution)/shard_map/ppermute | solution.py:19
  8.9 6.2 %collective-permute-start.9 = (bf16[20,32,128]{2,1,0:T(8,128)(2,1)}, bf16[20,32,128]{2,1,0:T(8,128)(2,1)}, u32[]{:S(2)}, u32[]{:S(2)}) collective-permute-start(bf16[20,32,128]{2,1,0:T(8,128)(2,1)} %get-tuple-element.8.u_ref), channel_id=1, source_target_pairs={{0,1},{1,2},{2,3},{3,4},{4,5},{5,6},{6,7},{8,9},{9,10},{10,11},{11... | collective-permute-start | bytes 491528 | tf_op jit(solution)/shard_map/ppermute | solution.py:19
  16.7 0.6 pad.51.fz
  17.4 2.2 %shard_map.100 = bf16[20,32,128]{2,1,0:T(8,128)(2,1)} custom-call(bf16[20,32,128]{2,1,0:T(8,128)(2,1)} %get-tuple-element.8.u_ref, bf16[32,32]{1,0:T(8,128)(2,1)} %pad.49.clone.fx, bf16[32,20]{1,0:T(8,128)(2,1)} %pad.50.clone.fy, bf16[128,128]{1,0:T(8,128)(2,1)} %pad.51.fz), custom_call_target="tpu_custom_call" | custom-call | tf_op jit(solution)/shard_map/pallas_call | solution.py:157
  20.1 0.6 pad.55.ex
  21.6 1.1 copy.38
  22.7 1.9 %convolution_bitcast_fusion.2 = bf16[12,4,20,5,20]{4,3,2,0,1:T(8,128)(2,1)} fusion(bf16[4,5,3,1,1]{1,2,4,3,0:T(4,128)(2,1)S(1)} %copy-done.9, bf16[3,12,20,20]{3,2,1,0:T(8,128)(2,1)S(1)} %copy-done.4), kind=kOutput, calls=%fused_computation.2 | convolution fusion | flops 576000 | bytes 220920 | tf_op jit(solution)/shard_map/tde,emli->mtldi/dot_general | solution.py:44
  24.7 0.7 convolution_bitcast_fusion.1
  25.7 1.6 %copy.44 = bf16[2,6,20,20,2,4]{2,4,0,3,5,1:T(2,128)(2,1)} copy(bf16[2,6,20,20,2,4]{3,5,2,0,1,4:T(4,128)(2,1)S(1)} %convolution_bitcast_fusion.3) | data formatting | bytes 153600 | tf_op jit(solution)/shard_map/qte,mf,egmlj->gmqlftj/dot_general | solution.py:48
  27.3 2.6 %multiply_bitcast_fusion = (bf16[6,2,2,20,2,4,20]{3,2,1,6,5,4,0:T(2,128)(2,1)S(1)}, bf16[6,2,2,20,2,4,20]{3,2,1,6,5,4,0:T(2,128)(2,1)S(1)}) fusion(bf16[2,6,20,20,2,4]{2,4,0,3,5,1:T(2,128)(2,1)} %copy.44, bf16[2,2]{0,1:T(2,128)(2,1)S(1)} %compare_convert_fusion, bf16[2,6,20,20,2,4]{2,4,0,3,5,1:T(2,128)(2,1)S(1)} %copy.38), kind=kLoop, calls=%fused_computation.7 | loop fusion | flops 153600 | bytes 460808 | tf_op jit(solution)/shard_map/qte,mf,egmlj->gmqlftj/transpose | solution.py:48
  29.9 2.1 %pad.59 = bf16[6,2,2,32,2,4,20]{3,2,1,6,5,4,0:T(2,128)(2,1)} pad(bf16[6,2,2,20,2,4,20]{3,2,1,6,5,4,0:T(2,128)(2,1)S(1)} %get-tuple-element.13, bf16[]{:T(256)} %constant.36.clone.1), padding=0_0x0_0x0_0x0_12x0_0x0_0x0_0 | pad | bytes 399362 | tf_op jit(solution)/shard_map/jit(_pad)/pad | solution.py:51
  32.0 2.8 %reshape.59 = bf16[6,128,160]{1,2,0:T(8,128)(2,1)S(1)} reshape(bf16[6,2,2,32,2,4,20]{3,2,1,6,5,4,0:T(2,128)(2,1)} %pad.59) | data formatting | bytes 491520 | tf_op jit(solution)/shard_map/reshape | solution.py:52
  34.8 0.9 copy.48.second
  36.8 2.0 %reshape.75.first = bf16[6,192,160]{2,1,0:T(8,128)(2,1)} reshape(bf16[12,4,24,5,32]{4,3,2,1,0:T(8,128)(2,1)S(1)} %pad.58.clone) | data formatting | bytes 737280 | tf_op jit(solution)/shard_map/reshape | solution.py:46
  38.8 1.6 %convolution_bitcast_fusion = bf16[12,2,4,20,4,20]{3,4,5,0,2,1:T(4,128)(2,1)S(1)} fusion(bf16[2,4,4,3,1,1]{3,2,5,4,1,0:T(4,128)(2,1)S(1)} %copy-done.10, bf16[3,12,20,20,1,1]{3,2,1,0,5,4:T(8,128)(2,1)} %bitcast.78), kind=kOutput, calls=%fused_computation | convolution fusion | flops 921600 | bytes 336192 | tf_op jit(solution)/shard_map/qzwe,emlk->mqzkwl/dot_general | solution.py:53
  40.4 4.3 %copy.46 = bf16[12,2,4,20,4,20]{5,4,3,2,1,0:T(4,128)(2,1)} copy(bf16[12,2,4,20,4,20]{3,4,5,0,2,1:T(4,128)(2,1)S(1)} %convolution_bitcast_fusion) | data formatting | bytes 614400 | tf_op jit(solution)/shard_map/qzwe,emlk->mqzkwl/transpose | solution.py:53
  44.8 2.9 %reshape.60 = bf16[24,80,80]{2,1,0:T(8,128)(2,1)S(1)} reshape(bf16[12,2,4,20,4,20]{5,4,3,2,1,0:T(4,128)(2,1)} %copy.46) | data formatting | bytes 614400 | tf_op jit(solution)/shard_map/reshape | solution.py:54
  47.7 1.1 pad.60
  48.8 2.1 %pad.53 = bf16[6,2,2,32,2,4,20]{3,2,1,6,5,4,0:T(2,128)(2,1)} pad(bf16[6,2,2,20,2,4,20]{3,2,1,6,5,4,0:T(2,128)(2,1)S(1)} %get-tuple-element.14, bf16[]{:T(256)} %constant.36.clone.1), padding=0_0x0_0x0_0x0_12x0_0x0_0x0_0 | pad | bytes 399362 | tf_op jit(solution)/shard_map/jit(_pad)/pad | solution.py:51
  51.0 3.0 %reshape.53 = bf16[6,128,160]{1,2,0:T(8,128)(2,1)S(1)} reshape(bf16[6,2,2,32,2,4,20]{3,2,1,6,5,4,0:T(2,128)(2,1)} %pad.53) | data formatting | bytes 491520 | tf_op jit(solution)/shard_map/reshape | solution.py:52
  54.0 0.9 copy.50.second
  55.0 0.6 pad.57.ez
  56.7 2.0 %reshape.74.first = bf16[6,192,160]{2,1,0:T(8,128)(2,1)} reshape(bf16[12,4,24,5,32]{4,3,2,1,0:T(8,128)(2,1)S(1)} %pad.52.clone) | data formatting | bytes 737280 | tf_op jit(solution)/shard_map/reshape | solution.py:46
  59.2 1.0 copy.40
  60.4 1.1 %pad.54 = bf16[24,128,128]{2,1,0:T(8,128)(2,1)} pad(bf16[24,40,40]{2,1,0:T(8,128)(2,1)S(1)} %reshape.54, bf16[]{:T(256)} %constant.36.clone.1), padding=0_0x0_88x0_88 | pad | bytes 863234 | tf_op jit(solution)/shard_map/jit(_pad)/pad | solution.py:55
  61.5 1.0 fusion
  62.5 2.0 %collective-permute-start.1 = (bf16[20,32,128]{2,1,0:T(8,128)(2,1)S(1)}, bf16[20,32,128]{2,1,0:T(8,128)(2,1)S(1)}, u32[]{:S(2)}, u32[]{:S(2)}) collective-permute-start(bf16[20,32,128]{2,1,0:T(8,128)(2,1)S(1)} %fusion), channel_id=1, source_target_pairs={{0,1},{1,0},{2,3},{3,2},{4,5},{5,4},{6,7},{7,6},{8,9},{9,8},{10,11... | collective-permute-start | bytes 491528 | tf_op jit(solution)/shard_map/ppermute | solution.py:24
  64.5 0.9 constant_dynamic-update-slice_fusion.8
  65.4 0.9 constant_dynamic-update-slice_fusion.7
  66.4 0.9 constant_dynamic-update-slice_fusion.6
  67.3 0.9 constant_dynamic-update-slice_fusion.5.u_ref
  68.3 1.1 collective-permute-done.1
  69.3 1.0 constant_dynamic-update-slice_fusion.4
  70.3 1.3 %collective-permute-start.2 = (bf16[20,32,128]{2,1,0:T(8,128)(2,1)S(1)}, bf16[20,32,128]{2,1,0:T(8,128)(2,1)S(1)}, u32[]{:S(2)}, u32[]{:S(2)}) collective-permute-start(bf16[20,32,128]{2,1,0:T(8,128)(2,1)S(1)} %get-tuple-element.6), channel_id=1, source_target_pairs={{2,0},{3,1},{4,2},{5,3},{6,4},{7,5},{10,8},{11,9},{12,10},{13,11},... | collective-permute-start | bytes 491528 | tf_op jit(solution)/shard_map/ppermute | solution.py:19
  71.6 4.6 %collective-permute-start.3 = (bf16[20,32,128]{2,1,0:T(8,128)(2,1)S(1)}, bf16[20,32,128]{2,1,0:T(8,128)(2,1)S(1)}, u32[]{:S(2)}, u32[]{:S(2)}) collective-permute-start(bf16[20,32,128]{2,1,0:T(8,128)(2,1)S(1)} %get-tuple-element.6), channel_id=1, source_target_pairs={{0,2},{1,3},{2,4},{3,5},{4,6},{5,7},{8,10},{9,11},{10,12},{11,13},... | collective-permute-start | bytes 491528 | tf_op jit(solution)/shard_map/ppermute | solution.py:19
  76.2 11.4 %shard_map.101.fine = f32[20,32,128]{2,1,0:T(8,128)} custom-call(bf16[20,160,128]{2,1,0:T(8,128)(2,1)} %copy-done.8, bf16[6,192,160]{2,1,0:T(8,128)(2,1)} %reshape.75.first, bf16[6,128,160]{2,1,0:T(8,128)(2,1)} %copy.48.second, bf16[3072,128]{1,0:T(8,128)(2,1)} %bitcast.83), custom_call_target="tpu_custom_call" | custom-call | flops 4000000000 | bytes 4000000 | tf_op jit(solution)/shard_map/pallas_call | solution.py:168
  87.6 1.3 %collective-permute-start.4 = (bf16[20,32,128]{2,1,0:T(8,128)(2,1)S(1)}, bf16[20,32,128]{2,1,0:T(8,128)(2,1)S(1)}, u32[]{:S(2)}, u32[]{:S(2)}) collective-permute-start(bf16[20,32,128]{2,1,0:T(8,128)(2,1)S(1)} %get-tuple-element.6), channel_id=1, source_target_pairs={{16,0},{24,8},{17,1},{25,9},{18,2},{26,10},{19,3},{27,11},{20,4},{... | collective-permute-start | bytes 491528 | tf_op jit(solution)/shard_map/ppermute | solution.py:19
  88.9 4.8 %collective-permute-start.5 = (bf16[20,32,128]{2,1,0:T(8,128)(2,1)S(1)}, bf16[20,32,128]{2,1,0:T(8,128)(2,1)S(1)}, u32[]{:S(2)}, u32[]{:S(2)}) collective-permute-start(bf16[20,32,128]{2,1,0:T(8,128)(2,1)S(1)} %get-tuple-element.6), channel_id=1, source_target_pairs={{0,16},{8,24},{1,17},{9,25},{2,18},{10,26},{3,19},{11,27},{4,20},{... | collective-permute-start | bytes 491528 | tf_op jit(solution)/shard_map/ppermute | solution.py:19
  93.8 1.0 collective-permute-done.4
  94.9 1.4 %collective-permute-done.5 = bf16[20,32,128]{2,1,0:T(8,128)(2,1)S(1)} collective-permute-done((bf16[20,32,128]{2,1,0:T(8,128)(2,1)S(1)}, bf16[20,32,128]{2,1,0:T(8,128)(2,1)S(1)}, u32[]{:S(2)}, u32[]{:S(2)}) %collective-permute-start.5) | collective-permute-done | bytes 163872 | tf_op jit(solution)/shard_map/ppermute | solution.py:19
  96.3 0.9 copy-done.3
  97.2 12.2 %shard_map.102 = f32[20,32,128]{2,1,0:T(8,128)} custom-call(bf16[20,160,128]{2,1,0:T(8,128)(2,1)} %copy-done.3, bf16[6,192,160]{2,1,0:T(8,128)(2,1)} %reshape.74.first, bf16[6,128,160]{2,1,0:T(8,128)(2,1)} %copy.50.second, bf16[3072,128]{1,0:T(8,128)(2,1)} %bitcast.77, bf16[32,32]{1,0:T(8,128)(2,1)} %pad.55.ex, bf16[32,20]{1,0:T(8,128)(2,1)} %pad.56.ey, ...), custom_call_target="tpu_custom_call" | custom-call | tf_op jit(solution)/shard_map/pallas_call | solution.py:175
  109.4 1.0 slice.4
  110.8 1.1 reshape.63
  (61 shorter events, 7.2 us)
Async XLA Ops:
  0.0 21.4 %copy-start.11 = (bf16[2,4,3,1,1,1]{2,1,5,4,3,0:T(4,128)(2,1)S(1)}, bf16[2,4,3,1,1,1]{2,1,5,4,3,0:T(4,128)(2,1)}, u32[]{:S(2)}) copy-start(bf16[2,4,3,1,1,1]{2,1,5,4,3,0:T(4,128)(2,1)} %constant.74) | copy-start | bytes 148
  0.0 15.1 %copy-start.6 = (bf16[2,20,20]{2,0,1:T(2,128)(2,1)S(1)}, bf16[2,20,20]{2,0,1:T(2,128)(2,1)}, u32[]{:S(2)}) copy-start(bf16[2,20,20]{2,0,1:T(2,128)(2,1)} %param.13) | copy-start | bytes 4804
  0.0 21.3 %copy-start.4 = (bf16[3,12,20,20]{3,2,1,0:T(8,128)(2,1)S(1)}, bf16[3,12,20,20]{3,2,1,0:T(8,128)(2,1)}, u32[]{:S(2)}) copy-start(bf16[3,12,20,20]{3,2,1,0:T(8,128)(2,1)} %param.12) | copy-start | bytes 86404
  1.6 21.1 %copy-start.9 = (bf16[4,5,3,1,1]{1,2,4,3,0:T(4,128)(2,1)S(1)}, bf16[4,5,3,1,1]{1,2,4,3,0:T(4,128)(2,1)}, u32[]{:S(2)}) copy-start(bf16[4,5,3,1,1]{1,2,4,3,0:T(4,128)(2,1)} %constant.73) | copy-start | bytes 364
  2.6 61.8 %collective-permute-start.6 = (bf16[20,32,128]{2,1,0:T(8,128)(2,1)}, bf16[20,32,128]{2,1,0:T(8,128)(2,1)}, u32[]{:S(2)}, u32[]{:S(2)}) collective-permute-start(bf16[20,32,128]{2,1,0:T(8,128)(2,1)} %get-tuple-element.8.u_ref), channel_id=1, source_target_pairs={{8,0},{16,8},{24,16},{9,1},{17,9},{25,17},{10,2},{18,10},{26,18},{... | collective-permute-start | bytes 491528 | tf_op jit(solution)/shard_map/ppermute | solution.py:19
  3.9 61.5 %collective-permute-start.7 = (bf16[20,32,128]{2,1,0:T(8,128)(2,1)}, bf16[20,32,128]{2,1,0:T(8,128)(2,1)}, u32[]{:S(2)}, u32[]{:S(2)}) collective-permute-start(bf16[20,32,128]{2,1,0:T(8,128)(2,1)} %get-tuple-element.8.u_ref), channel_id=1, source_target_pairs={{0,8},{8,16},{16,24},{1,9},{9,17},{17,25},{2,10},{10,18},{18,26},{... | collective-permute-start | bytes 491528 | tf_op jit(solution)/shard_map/ppermute | solution.py:19
  7.6 58.7 %collective-permute-start.8 = (bf16[20,32,128]{2,1,0:T(8,128)(2,1)}, bf16[20,32,128]{2,1,0:T(8,128)(2,1)}, u32[]{:S(2)}, u32[]{:S(2)}) collective-permute-start(bf16[20,32,128]{2,1,0:T(8,128)(2,1)} %get-tuple-element.8.u_ref), channel_id=1, source_target_pairs={{1,0},{2,1},{3,2},{4,3},{5,4},{6,5},{7,6},{9,8},{10,9},{11,10},{12... | collective-permute-start | bytes 491528 | tf_op jit(solution)/shard_map/ppermute | solution.py:19
  8.9 58.4 %collective-permute-start.9 = (bf16[20,32,128]{2,1,0:T(8,128)(2,1)}, bf16[20,32,128]{2,1,0:T(8,128)(2,1)}, u32[]{:S(2)}, u32[]{:S(2)}) collective-permute-start(bf16[20,32,128]{2,1,0:T(8,128)(2,1)} %get-tuple-element.8.u_ref), channel_id=1, source_target_pairs={{0,1},{1,2},{2,3},{3,4},{4,5},{5,6},{6,7},{8,9},{9,10},{10,11},{11... | collective-permute-start | bytes 491528 | tf_op jit(solution)/shard_map/ppermute | solution.py:19
  19.5 42.0 %collective-permute-start = (bf16[20,32,128]{2,1,0:T(8,128)(2,1)}, bf16[20,32,128]{2,1,0:T(8,128)(2,1)}, u32[]{:S(2)}, u32[]{:S(2)}) collective-permute-start(bf16[20,32,128]{2,1,0:T(8,128)(2,1)} %shard_map.100), channel_id=1, source_target_pairs={{0,8},{8,0},{16,24},{24,16},{1,9},{9,1},{17,25},{25,17},{2,10},{10... | collective-permute-start | bytes 491528 | tf_op jit(solution)/shard_map/ppermute | solution.py:24
  21.4 3.3 %copy-start.1 = (bf16[3,12,20,20]{3,2,1,0:T(8,128)(2,1)S(1)}, bf16[3,12,20,20]{3,2,1,0:T(8,128)(2,1)}, u32[]{:S(2)}) copy-start(bf16[3,12,20,20]{3,2,1,0:T(8,128)(2,1)} %param.11) | copy-start | bytes 86404
  36.8 2.0 %copy-start.10 = (bf16[2,4,4,3,1,1]{3,2,5,4,1,0:T(4,128)(2,1)S(1)}, bf16[2,4,4,3,1,1]{3,2,5,4,1,0:T(4,128)(2,1)}, u32[]{:S(2)}) copy-start(bf16[2,4,4,3,1,1]{3,2,5,4,1,0:T(4,128)(2,1)} %constant.76) | copy-start | bytes 580
  48.8 6.8 %copy-start = (bf16[12,4,20,5,20]{4,3,2,0,1:T(8,128)(2,1)S(1)}, bf16[12,4,20,5,20]{4,3,2,0,1:T(8,128)(2,1)}, u32[]{:S(2)}) copy-start(bf16[12,4,20,5,20]{4,3,2,0,1:T(8,128)(2,1)} %convolution_bitcast_fusion.2) | copy-start | bytes 576004
  56.7 2.0 %copy-start.5 = (bf16[3,12,20,20]{3,2,1,0:T(8,128)(2,1)S(1)}, bf16[3,12,20,20]{3,2,1,0:T(8,128)(2,1)}, u32[]{:S(2)}) copy-start(bf16[3,12,20,20]{3,2,1,0:T(8,128)(2,1)} %param.12) | copy-start | bytes 86404
  56.7 2.0 %copy-start.12 = (bf16[2,2,2,3,1,1]{3,2,5,4,1,0:T(2,128)(2,1)S(1)}, bf16[2,2,2,3,1,1]{3,2,5,4,1,0:T(2,128)(2,1)}, u32[]{:S(2)}) copy-start(bf16[2,2,2,3,1,1]{3,2,5,4,1,0:T(2,128)(2,1)} %constant.75) | copy-start | bytes 148
  58.7 2.8 %copy-start.2 = (bf16[20,32,128]{2,1,0:T(8,128)(2,1)S(1)}, bf16[20,32,128]{2,1,0:T(8,128)(2,1)}, u32[]{:S(2)}) copy-start(bf16[20,32,128]{2,1,0:T(8,128)(2,1)} %shard_map.100) | copy-start | bytes 491524
  58.7 5.8 %copy-start.7 = (bf16[20,160,128]{2,1,0:T(8,128)(2,1)S(1)}, bf16[20,160,128]{2,1,0:T(8,128)(2,1)}, u32[]{:S(2)}) copy-start(bf16[20,160,128]{2,1,0:T(8,128)(2,1)} %get-tuple-element.7) | copy-start | bytes 2457604
  62.5 6.8 %collective-permute-start.1 = (bf16[20,32,128]{2,1,0:T(8,128)(2,1)S(1)}, bf16[20,32,128]{2,1,0:T(8,128)(2,1)S(1)}, u32[]{:S(2)}, u32[]{:S(2)}) collective-permute-start(bf16[20,32,128]{2,1,0:T(8,128)(2,1)S(1)} %fusion), channel_id=1, source_target_pairs={{0,1},{1,0},{2,3},{3,2},{4,5},{5,4},{6,7},{7,6},{8,9},{9,8},{10,11... | collective-permute-start | bytes 491528 | tf_op jit(solution)/shard_map/ppermute | solution.py:24
  68.3 7.9 %copy-start.8 = (bf16[20,160,128]{2,1,0:T(8,128)(2,1)}, bf16[20,160,128]{2,1,0:T(8,128)(2,1)S(1)}, u32[]{:S(2)}) copy-start(bf16[20,160,128]{2,1,0:T(8,128)(2,1)S(1)} %constant_dynamic-update-slice_fusion.5.u_ref) | copy-start | bytes 2457604
  70.3 23.4 %collective-permute-start.2 = (bf16[20,32,128]{2,1,0:T(8,128)(2,1)S(1)}, bf16[20,32,128]{2,1,0:T(8,128)(2,1)S(1)}, u32[]{:S(2)}, u32[]{:S(2)}) collective-permute-start(bf16[20,32,128]{2,1,0:T(8,128)(2,1)S(1)} %get-tuple-element.6), channel_id=1, source_target_pairs={{2,0},{3,1},{4,2},{5,3},{6,4},{7,5},{10,8},{11,9},{12,10},{13,11},... | collective-permute-start | bytes 491528 | tf_op jit(solution)/shard_map/ppermute | solution.py:19
  71.6 22.1 %collective-permute-start.3 = (bf16[20,32,128]{2,1,0:T(8,128)(2,1)S(1)}, bf16[20,32,128]{2,1,0:T(8,128)(2,1)S(1)}, u32[]{:S(2)}, u32[]{:S(2)}) collective-permute-start(bf16[20,32,128]{2,1,0:T(8,128)(2,1)S(1)} %get-tuple-element.6), channel_id=1, source_target_pairs={{0,2},{1,3},{2,4},{3,5},{4,6},{5,7},{8,10},{9,11},{10,12},{11,13},... | collective-permute-start | bytes 491528 | tf_op jit(solution)/shard_map/ppermute | solution.py:19
  87.6 7.2 %collective-permute-start.4 = (bf16[20,32,128]{2,1,0:T(8,128)(2,1)S(1)}, bf16[20,32,128]{2,1,0:T(8,128)(2,1)S(1)}, u32[]{:S(2)}, u32[]{:S(2)}) collective-permute-start(bf16[20,32,128]{2,1,0:T(8,128)(2,1)S(1)} %get-tuple-element.6), channel_id=1, source_target_pairs={{16,0},{24,8},{17,1},{25,9},{18,2},{26,10},{19,3},{27,11},{20,4},{... | collective-permute-start | bytes 491528 | tf_op jit(solution)/shard_map/ppermute | solution.py:19
  88.9 7.4 %collective-permute-start.5 = (bf16[20,32,128]{2,1,0:T(8,128)(2,1)S(1)}, bf16[20,32,128]{2,1,0:T(8,128)(2,1)S(1)}, u32[]{:S(2)}, u32[]{:S(2)}) collective-permute-start(bf16[20,32,128]{2,1,0:T(8,128)(2,1)S(1)} %get-tuple-element.6), channel_id=1, source_target_pairs={{0,16},{8,24},{1,17},{9,25},{2,18},{10,26},{3,19},{11,27},{4,20},{... | collective-permute-start | bytes 491528 | tf_op jit(solution)/shard_map/ppermute | solution.py:19
  96.3 0.9 copy-start.3
where the time goes:
time: 113 us; the launch traced here: 112 us
  local copies, waits for them, and re-layouts  45.5 us (40%)
  starting transfers between devices  26.8 us (24%)
  Pallas kernels  25.7 us (23%)
  matrix products  5.26 us (5%)
  other arithmetic  4.64 us (4%)
  waiting for transfers between devices  3.51 us (3%)
    ppermute x8, starting transfers between devices, shifted(): return lax.ppermute(block, axis, route)  24.4 us
    pallas_call x1, Pallas kernels, shards(): pl.pallas_call(coarse_kernel, out_shape=jax.ShapeDtypeStruct((n, SUB, LAN...  12.2 us
    pallas_call x1, Pallas kernels, shards(): pl.pallas_call(fine_kernel, out_shape=jax.ShapeDtypeStruct((n, SUB, LANES...  11.4 us
    reshape x4, local copies, waits for them, and re-layouts, level_mats(): second = second.reshape(groups, PAIR * 2 * SUB, PAIR * 4 * n)  7.67 us
    unnamed x36, local copies, waits for them, and re-layouts  5.55 us
    transpose x2, local copies, waits for them, and re-layouts, level_mats(): third = jnp.einsum('qzwe,emlk->mqzkwl', jnp.asarray(sel_z, BF), blocks)  5.34 us
    pad x2, local copies, waits for them, and re-layouts, level_mats(): second = jnp.pad(second, ((0, 0),) * 3 + ((0, SUB - n),) + ((0, 0),) * 3)  4.26 us
    reshape x2, local copies, waits for them, and re-layouts, level_mats(): first = first.reshape(groups, PAIR * 4 * 24, 5 * SUB)  4 us
  transfers between devices with their start and end apart: 10, of which 3 were waited for; matrix products, arithmetic and copies ran while one was open for 43% of the time, Pallas kernels for 12%

commit v1 on v0

v1 whole, which is shorter than its diff:
```python
import functools

import jax
import jax.numpy as jnp
from jax import lax
from jax.experimental import pallas as pl
from jax.experimental.pallas import tpu as pltpu
from jax.sharding import PartitionSpec as P

BF = jnp.bfloat16
F32 = jnp.float32
PAIR = 2
SUB = 32
LANES = 128


def shifted(block, axis, distance):
    devices = range(lax.axis_size(axis))
    route = [(i - distance, i) for i in devices if i - distance in devices]
    return lax.ppermute(block, axis, route)


def partner(block, axis):
    count = lax.axis_size(axis)
    return lax.ppermute(block, axis, [(i, i ^ 1) for i in range(count)])


TROW = 24


def spread(rows, boxes, n):
    r = lax.broadcasted_iota(jnp.int32, (rows, LANES), 0)
    c = lax.broadcasted_iota(jnp.int32, (rows, LANES), 1)
    return jnp.where((lax.rem(c, n) == r) & (c < boxes * n), 1.0, 0.0).astype(BF)


def spread_t(cols, boxes, n):
    r = lax.broadcasted_iota(jnp.int32, (LANES, cols), 0)
    c = lax.broadcasted_iota(jnp.int32, (LANES, cols), 1)
    return jnp.where((lax.rem(r, n) == c) & (r < boxes * n), 1.0, 0.0).astype(BF)


def box_of(n):
    r = lax.broadcasted_iota(jnp.int32, (LANES, LANES), 0)
    c = lax.broadcasted_iota(jnp.int32, (LANES, LANES), 1)
    return lax.div(r, n), lax.div(c, n)


def tiled(padded, pieces, boxes_in, boxes_out, n):
    wide = dot(padded[:, :SUB].astype(BF), spread(SUB, boxes_in, n)).astype(BF)
    left = spread_t(TROW, boxes_out, n)
    return [dot(left, wide[p * TROW : (p + 1) * TROW]) for p in range(pieces)]


def level_mats(blk, pad, first, second, third, boxes):
    count, n, _ = blk.shape
    terms = count // 3
    pad[...] = jnp.zeros_like(pad)
    second[...] = jnp.zeros_like(second)
    for p in range(count):
        pad[p * TROW : p * TROW + n, :n] = blk[p].astype(F32)
    zero = jnp.zeros((TROW, LANES), F32)
    row, col = box_of(n)
    wide = tiled(pad[...], count, boxes, boxes, n)
    for m in range(terms):
        g, f = divmod(m, PAIR)
        low, mid, up = (pad[(e * terms + m) * TROW : (e * terms + m + 1) * TROW, :] for e in range(3))
        main = mid + pltpu.roll(up, SUB, 1) + pltpu.roll(low, 2 * SUB, 1)
        third_slot = pltpu.roll(mid, 3 * SUB, 1)
        at = f * 4 * TROW
        for t, (x, y) in enumerate([(main, zero), (third_slot, zero), (zero, mid), (mid, zero)]):
            first[g, at + t * TROW : at + (t + 1) * TROW, :LANES] = x
            first[g, at + t * TROW : at + (t + 1) * TROW, LANES:] = y
        at = f * 2 * SUB
        second[g, at : at + TROW, f * LANES : (f + 1) * LANES] = main
        second[g, at + SUB : at + SUB + TROW, f * LANES : (f + 1) * LANES] = third_slot
        at = m * 2 * LANES
        third[:, at : at + LANES] = jnp.where(row == col, wide[terms + m], 0.0).astype(BF)
        third[:, at + LANES : at + 2 * LANES] = (
            jnp.where(col == row + 1, wide[2 * terms + m], 0.0)
            + jnp.where(col == row - 1, wide[m], 0.0)
        ).astype(BF)


def pair_mats(mats, pad, boxes_in, boxes_out, n):
    row, col = box_of(n)
    fine, parent = (col, row) if boxes_in > boxes_out else (row, col)
    for c in range(2):
        pad[c * TROW : c * TROW + n, :n] = mats[c].astype(F32)
    wide = tiled(pad[: 2 * TROW, :], 2, boxes_in, boxes_out, n)
    keep = lax.div(fine, 2) == parent
    even = lax.rem(fine, 2) == 0
    return jnp.where(keep, jnp.where(even, wide[0], wide[1]), 0.0).astype(BF)


def small(mat, pad, at):
    n = mat.shape[0]
    pad[at * SUB : at * SUB + n, :n] = mat.astype(F32)
    return pad[at * SUB : (at + 1) * SUB, :SUB].astype(BF)


def dot_t(a, b):
    return lax.dot_general(a, b, (((1,), (1,)), ((), ())), preferred_element_type=F32)


def dot(a, b):
    return jnp.dot(a, b, preferred_element_type=F32)


def level(u, first, second, third, flip, mid, n):
    groups = first.shape[0]
    width = PAIR * 4 * SUB
    for g in range(groups):
        slot = flip.at[g % 2]
        lhs = first[g][:, : 5 * SUB].astype(BF)
        for j in range(0, n, 2):
            a = dot(lhs, jnp.concatenate([u(j), u(j + 1)], axis=1))
            for h in range(2):
                for t in range(PAIR * 4):
                    slot[pl.ds(t * SUB + j + h, n, stride=width), :] = a[
                        t * TROW : t * TROW + n, h * LANES : (h + 1) * LANES
                    ]
        lhs = second[g].astype(BF)
        for l in range(0, n, 2):
            rhs = jnp.concatenate(
                [slot[l * width : (l + 1) * width, :], slot[(l + 1) * width : (l + 2) * width, :]],
                axis=1,
            ).astype(BF)
            b = dot(lhs, rhs).astype(BF)
            for h in range(2):
                for q in range(PAIR * 2):
                    at = (g * PAIR * 2 + q) * LANES
                    mid[(l + h) * SUB : (l + h + 1) * SUB, at : at + LANES] = b[
                        q * SUB : (q + 1) * SUB, h * LANES : (h + 1) * LANES
                    ]
    return dot_t(mid[...], third[...])


def single(u, first, second, third, slot, mid, n):
    for j in range(0, n, 2):
        a = dot(first, jnp.concatenate([u(j), u(j + 1)], axis=1))
        for h in range(2):
            slot[pl.ds(j + h, n, stride=SUB), :] = a[:n, h * LANES : (h + 1) * LANES]
    for l in range(0, n, 2):
        rhs = jnp.concatenate(
            [slot[l * SUB : l * SUB + n, :], slot[(l + 1) * SUB : (l + 1) * SUB + n, :]], axis=1
        ).astype(BF)
        b = dot(second[:, :n], rhs).astype(BF)
        for h in range(2):
            mid[(l + h) * SUB : (l + h + 1) * SUB, :LANES] = b[:, h * LANES : (h + 1) * LANES]
    return dot_t(mid[:, :LANES], third)


def filter_kernel(px, py, u_ref, filters, out, flip, mid, spare, boxes):
    n = u_ref.shape[0]
    spare[...] = jnp.zeros_like(spare)
    fx, fy = small(filters[px[0]], spare, 0), small(filters[py[0]], spare, 1)
    spare[...] = jnp.zeros_like(spare)
    fz = pair_mats(filters, spare, boxes, boxes // 2, n)
    s = single(lambda j: u_ref[j], fx, fy, fz, flip.at[0], mid, n)
    out[...] = s.reshape(n, SUB, LANES).astype(out.dtype)


def fine_kernel(u_ref, blk, out, flip, mid, pad, first, second, third, boxes):
    n = u_ref.shape[0]
    flip[...] = jnp.zeros_like(flip)
    level_mats(blk, pad, first, second, third, boxes)
    out[...] = level(lambda j: u_ref[j], first, second, third, flip, mid, n).reshape(out.shape)


def coarse_kernel(
    px, py, u_ref, blk, turned, fine, out, flip, mid, pad, first, second, third, res, spare, boxes
):
    n = u_ref.shape[0]
    flip[...] = jnp.zeros_like(flip)
    level_mats(blk, pad, first, second, third, boxes // 2)
    s = level(lambda j: u_ref[j], first, second, third, flip, mid, n)
    res[...] = s.reshape(n, SUB, LANES).astype(BF)
    spare[...] = jnp.zeros_like(spare)
    ex, ey = small(turned[px[0]], spare, 0), small(turned[py[0]], spare, 1)
    spare[...] = jnp.zeros_like(spare)
    ez = pair_mats(turned, spare, boxes // 2, boxes, n)
    s = single(lambda j: res[j], ex, ey, ez, flip.at[0], mid, n)
    out[...] = fine[...] + s.reshape(out.shape)


def scratch(n, terms, whole=True):
    out = [
        pltpu.VMEM((2, n * PAIR * 4 * SUB, LANES), F32),
        pltpu.VMEM((n * SUB, terms * 2 * LANES), BF),
    ]
    if whole:
        groups = terms // PAIR
        out += [
            pltpu.VMEM((3 * terms * TROW, LANES), F32),
            pltpu.VMEM((groups, PAIR * 4 * TROW, 2 * LANES), F32),
            pltpu.VMEM((groups, PAIR * 2 * SUB, 2 * LANES), F32),
            pltpu.VMEM((LANES, terms * 2 * LANES), BF),
        ]
    return out


VM = pl.BlockSpec(memory_space=pltpu.VMEM)
SM = pl.BlockSpec(memory_space=pltpu.SMEM)
SPARE = pltpu.VMEM((2 * SUB, LANES), F32)
PARAMS = pltpu.CompilerParams(vmem_limit_bytes=60 * 1024 * 1024)


def shards(fine_source, fine_blocks, coarse_blocks, filters):
    boxes = fine_source.shape[2]
    terms, n = fine_blocks.shape[1], fine_blocks.shape[2]
    raw = fine_source.reshape(boxes, n, n, n)
    own = raw.transpose(2, 1, 0, 3).reshape(n, n, boxes * n)
    own = jnp.pad(own, ((0, 0), (0, SUB - n), (0, LANES - boxes * n)))
    parity_x = lax.axis_index("gx") % 2
    parity_y = lax.axis_index("gy") % 2
    px, py = parity_x.reshape(1), parity_y.reshape(1)
    turned = filters.swapaxes(1, 2)
    grid_out = jax.ShapeDtypeStruct((n, SUB, LANES), BF)
    partial = pl.pallas_call(
        functools.partial(filter_kernel, boxes=boxes),
        out_shape=grid_out,
        in_specs=[SM, SM, VM, VM],
        out_specs=VM,
        scratch_shapes=scratch(n, terms, False) + [SPARE],
        compiler_params=PARAMS,
    )(px, py, own, filters)
    sides = [shifted(own, "gx", -1), shifted(own, "gx", 1)]
    sides += [shifted(own, "gy", -1), shifted(own, "gy", 1)]
    fine_u = jnp.concatenate([own] + sides, axis=1)
    half = partial.astype(F32) + partner(partial, "gx").astype(F32)
    parent = (half + partner(half.astype(BF), "gy").astype(F32)).astype(BF)
    near = [shifted(parent, "gy", -2), shifted(parent, "gy", 2)]
    near += [shifted(parent, "gx", -2), shifted(parent, "gx", 2)]
    coarse_u = jnp.concatenate([parent] + near, axis=1)
    fine = pl.pallas_call(
        functools.partial(fine_kernel, boxes=boxes),
        out_shape=jax.ShapeDtypeStruct((n, SUB, LANES), F32),
        scratch_shapes=scratch(n, terms),
        compiler_params=PARAMS,
        cost_estimate=pl.CostEstimate(flops=4_000_000_000, bytes_accessed=4_000_000, transcendentals=0),
    )(fine_u, fine_blocks.reshape(3 * terms, n, n))
    out = pl.pallas_call(
        functools.partial(coarse_kernel, boxes=boxes),
        in_specs=[SM, SM, VM, VM, VM, VM],
        out_specs=VM,
        out_shape=jax.ShapeDtypeStruct((n, SUB, LANES), F32),
        scratch_shapes=scratch(n, terms) + [pltpu.VMEM((n, SUB, LANES), BF), SPARE],
        compiler_params=PARAMS,
    )(px, py, coarse_u, coarse_blocks.reshape(3 * terms, n, n), turned, fine)
    out = out[:, :n, : boxes * n].reshape(n, n, boxes, n).transpose(2, 0, 1, 3)
    return out.reshape(1, 1, boxes, n * n * n)


def solution(mesh):
    in_specs = (P("gx", "gy", None, None), P(), P(), P())
    out_specs = P("gx", "gy", None, None)
    return jax.shard_map(shards, mesh=mesh, in_specs=in_specs, out_specs=out_specs, check_vma=False)
```

time: 113 us -> 70.5 us (0.62)
  local copies, waits for them, and re-layouts: 45.5 us -> 7.28 us
  waiting for transfers between devices: 3.51 us -> 8.95 us
  matrix products: 5.26 us -> 0 us
  other arithmetic: 4.64 us -> 1.03 us
  Pallas kernels: 25.7 us -> 27.2 us
  starting transfers between devices: 26.8 us -> 25.4 us
    reshape x11 -> x0, local copies, waits for them, and re-layouts: 15.1 us -> none  [the longest x4 7.67 us: level_mats(): second = second.reshape(groups, PAIR * 2 * SUB, PAIR * 4 * n)]
    pad x12 -> x0, local copies, waits for them, and re-layouts: 11.3 us -> none  [the longest x2 4.26 us: level_mats(): second = jnp.pad(second, ((0, 0),) * 3 + ((0, SUB - n),) + ((0, 0),) * 3)]
    transpose x2 -> x0, local copies, waits for them, and re-layouts: 5.34 us -> none  [level_mats(): third = jnp.einsum('qzwe,emlk->mqzkwl', jnp.asarray(sel_z, BF), blocks)]
    dot_general x6 -> x0, matrix products: 5.26 us -> none  [the longest x2 2.67 us: level_mats(): first = jnp.einsum('tde,emli->mtldi', jnp.asarray(SEL_X, BF), blocks)]
    ppermute x8, waiting for transfers between devices: 2.45 us -> 5.67 us  [shifted(): return lax.ppermute(block, axis, route)]
    transpose x2 -> x0, other arithmetic: 2.69 us -> none  [the longest x1 2.57 us: level_mats(): jnp.einsum('qte,mf,egmlj->gmqlftj', jnp.asarray(SEL_Y, BF), jnp.eye(PAIR,...]
    dot_general x2 -> x0, local copies, waits for them, and re-layouts: 2.66 us -> none  [level_mats(): jnp.einsum('qte,mf,egmlj->gmqlftj', jnp.asarray(SEL_Y, BF), jnp.eye(PAIR,...]
    ppermute x2, waiting for transfers between devices: 1.06 us -> 3.28 us  [partner(): return lax.ppermute(block, axis, [(i, i ^ 1) for i in range(count)])]
  transfers between devices with their start and end apart: 10 -> 10, of which waited for: 3 -> 2; matrix products, arithmetic and copies ran while one was open for 43% -> 3% of each run, Pallas kernels for 12% -> 17%
where the time goes in v1:
time: 70.5 us; the launch traced here: 70 us
  Pallas kernels  27.2 us (39%)
  starting transfers between devices  25.4 us (36%)
  waiting for transfers between devices  8.95 us (13%)
  local copies, waits for them, and re-layouts  7.28 us (10%)
  other arithmetic  1.03 us (1%)
    ppermute x8, starting transfers between devices, shifted(): return lax.ppermute(block, axis, route)  22.4 us
    pallas_call x1, Pallas kernels, shards(): pl.pallas_call(functools.partial(coarse_kernel, boxes=boxes), in_specs=[S...  12.8 us
    pallas_call x1, Pallas kernels, shards(): pl.pallas_call(functools.partial(fine_kernel, boxes=boxes), out_shape=jax...  11.9 us
    ppermute x8, waiting for transfers between devices, shifted(): return lax.ppermute(block, axis, route)  5.67 us
    unnamed x21, local copies, waits for them, and re-layouts  3.78 us
    ppermute x2, waiting for transfers between devices, partner(): return lax.ppermute(block, axis, [(i, i ^ 1) for i in range(count)])  3.28 us
    ppermute x2, starting transfers between devices, partner(): return lax.ppermute(block, axis, [(i, i ^ 1) for i in range(count)])  2.92 us
    pallas_call x1, Pallas kernels, shards(): pl.pallas_call(functools.partial(filter_kernel, boxes=boxes), out_shape=g...  2.39 us
  transfers between devices with their start and end apart: 10, of which 2 were waited for; matrix products, arithmetic and copies ran while one was open for 3% of the time, Pallas kernels for 17%

profile of v1, /device:TPU:0, one launch (start us, length us, event | category | flops | bytes accessed | tf_op | source)
XLA Modules:
  0.0 70.0 jit_solution(13487544349053474121)
XLA Ops:
  0.0 0.0 copy-start.3
  0.0 1.3 %copy.10.filters = bf16[2,20,20]{2,1,0:T(8,128)(2,1)} copy(bf16[2,20,20]{2,0,1:T(2,128)(2,1)} %param.7) | data formatting | bytes 3200 | tf_op args[3]
  1.3 0.0 copy-done.3
  1.3 0.5 reshape.26
  1.8 0.2 copy.9
  2.0 0.2 reshape.27
  2.3 0.7 %constant_dynamic-update-slice_fusion.9 = (bf16[20,160,128]{2,1,0:T(8,128)(2,1)S(1)}, bf16[20,32,128]{2,1,0:T(8,128)(2,1)}) fusion(bf16[20,20,80]{2,1,0:T(8,128)(2,1)S(1)} %reshape.27), kind=kLoop, calls=%fused_computation.13 | loop fusion | bytes 391680
  3.0 0.0 copy-start.2
  3.0 0.0 copy-start.4
  3.0 2.4 %shard_map.46 = bf16[20,32,128]{2,1,0:T(8,128)(2,1)} custom-call(s32[1]{0:T(128)} %bitcast.px, s32[1]{0:T(128)} %bitcast.1.py, bf16[20,32,128]{2,1,0:T(8,128)(2,1)} %get-tuple-element.8.u_ref, bf16[2,20,20]{2,1,0:T(8,128)(2,1)} %copy.10.filters), custom_call_target="tpu_custom_call" | custom-call | tf_op jit(solution)/shard_map/pallas_call | solution.py:220
  5.4 0.5 collective-permute-start
  5.9 0.0 copy-done.2
  5.9 4.4 %collective-permute-start.9 = (bf16[20,32,128]{2,1,0:T(8,128)(2,1)S(1)}, bf16[20,32,128]{2,1,0:T(8,128)(2,1)S(1)}, u32[]{:S(2)}, u32[]{:S(2)}) collective-permute-start(bf16[20,32,128]{2,1,0:T(8,128)(2,1)S(1)} %copy-done.2), channel_id=1, source_target_pairs={{0,1},{1,2},{2,3},{3,4},{4,5},{5,6},{6,7},{8,9},{9,10},{10,11},{11... | collective-permute-start | bytes 491528 | tf_op jit(solution)/shard_map/ppermute | solution.py:20
  10.3 1.3 %collective-permute-start.8 = (bf16[20,32,128]{2,1,0:T(8,128)(2,1)S(1)}, bf16[20,32,128]{2,1,0:T(8,128)(2,1)S(1)}, u32[]{:S(2)}, u32[]{:S(2)}) collective-permute-start(bf16[20,32,128]{2,1,0:T(8,128)(2,1)S(1)} %copy-done.2), channel_id=1, source_target_pairs={{1,0},{2,1},{3,2},{4,3},{5,4},{6,5},{7,6},{9,8},{10,9},{11,10},{12... | collective-permute-start | bytes 491528 | tf_op jit(solution)/shard_map/ppermute | solution.py:20
  11.6 2.1 %collective-permute-start.7 = (bf16[20,32,128]{2,1,0:T(8,128)(2,1)S(1)}, bf16[20,32,128]{2,1,0:T(8,128)(2,1)S(1)}, u32[]{:S(2)}, u32[]{:S(2)}) collective-permute-start(bf16[20,32,128]{2,1,0:T(8,128)(2,1)S(1)} %copy-done.2), channel_id=1, source_target_pairs={{0,8},{8,16},{16,24},{1,9},{9,17},{17,25},{2,10},{10,18},{18,26},{... | collective-permute-start | bytes 491528 | tf_op jit(solution)/shard_map/ppermute | solution.py:20
  13.7 1.3 %collective-permute-start.6 = (bf16[20,32,128]{2,1,0:T(8,128)(2,1)S(1)}, bf16[20,32,128]{2,1,0:T(8,128)(2,1)S(1)}, u32[]{:S(2)}, u32[]{:S(2)}) collective-permute-start(bf16[20,32,128]{2,1,0:T(8,128)(2,1)S(1)} %copy-done.2), channel_id=1, source_target_pairs={{8,0},{16,8},{24,16},{9,1},{17,9},{25,17},{10,2},{18,10},{26,18},{... | collective-permute-start | bytes 491528 | tf_op jit(solution)/shard_map/ppermute | solution.py:20
  15.0 0.0 copy-done.4
  15.0 0.7 %copy.11 = bf16[2,20,20]{1,2,0:T(8,128)(2,1)} copy(bf16[2,20,20]{2,0,1:T(2,128)(2,1)S(1)} %copy-done.4) | data formatting | bytes 3200 | tf_op args[3]
  15.8 0.0 collective-permute-done
  15.8 1.0 %fusion = bf16[20,32,128]{2,1,0:T(8,128)(2,1)S(1)} fusion(bf16[20,32,128]{2,1,0:T(8,128)(2,1)S(1)} %collective-permute-done, bf16[20,32,128]{2,1,0:T(8,128)(2,1)} %shard_map.46), kind=kLoop, calls=%fused_computation.3 | loop fusion | flops 327680 | bytes 491520 | tf_op jit(solution)/shard_map/convert_element_type | solution.py:232
  16.7 2.4 %collective-permute-start.1 = (bf16[20,32,128]{2,1,0:T(8,128)(2,1)S(1)}, bf16[20,32,128]{2,1,0:T(8,128)(2,1)S(1)}, u32[]{:S(2)}, u32[]{:S(2)}) collective-permute-start(bf16[20,32,128]{2,1,0:T(8,128)(2,1)S(1)} %fusion), channel_id=1, source_target_pairs={{0,1},{1,0},{2,3},{3,2},{4,5},{5,4},{6,7},{7,6},{8,9},{9,8},{10,11... | collective-permute-start | bytes 491528 | tf_op jit(solution)/shard_map/ppermute | solution.py:25
  19.2 0.0 collective-permute-done.6
  19.2 0.0 collective-permute-done.7
  19.2 0.0 collective-permute-done.8
  19.3 0.0 copy-start
  19.3 0.0 collective-permute-done.9
  19.3 0.0 copy-start.5
  19.3 3.3 %collective-permute-done.1 = bf16[20,32,128]{2,1,0:T(8,128)(2,1)S(1)} collective-permute-done((bf16[20,32,128]{2,1,0:T(8,128)(2,1)S(1)}, bf16[20,32,128]{2,1,0:T(8,128)(2,1)S(1)}, u32[]{:S(2)}, u32[]{:S(2)}) %collective-permute-start.1) | collective-permute-done | bytes 163872 | tf_op jit(solution)/shard_map/ppermute | solution.py:25
  22.6 0.0 copy-done
  22.6 0.1 constant_dynamic-update-slice_fusion.4
  22.7 5.2 %collective-permute-start.3 = (bf16[20,32,128]{2,1,0:T(8,128)(2,1)S(1)}, bf16[20,32,128]{2,1,0:T(8,128)(2,1)S(1)}, u32[]{:S(2)}, u32[]{:S(2)}) collective-permute-start(bf16[20,32,128]{2,1,0:T(8,128)(2,1)S(1)} %get-tuple-element.6), channel_id=1, source_target_pairs={{0,2},{1,3},{2,4},{3,5},{4,6},{5,7},{8,10},{9,11},{10,12},{11,13},... | collective-permute-start | bytes 491528 | tf_op jit(solution)/shard_map/ppermute | solution.py:20
  27.9 1.3 %collective-permute-start.2 = (bf16[20,32,128]{2,1,0:T(8,128)(2,1)S(1)}, bf16[20,32,128]{2,1,0:T(8,128)(2,1)S(1)}, u32[]{:S(2)}, u32[]{:S(2)}) collective-permute-start(bf16[20,32,128]{2,1,0:T(8,128)(2,1)S(1)} %get-tuple-element.6), channel_id=1, source_target_pairs={{2,0},{3,1},{4,2},{5,3},{6,4},{7,5},{10,8},{11,9},{12,10},{13,11},... | collective-permute-start | bytes 491528 | tf_op jit(solution)/shard_map/ppermute | solution.py:20
  29.2 0.0 copy-done.5
  29.2 11.9 %shard_map.47.fine = f32[20,32,128]{2,1,0:T(8,128)} custom-call(bf16[20,160,128]{2,1,0:T(8,128)(2,1)} %copy-done.5, bf16[36,20,20]{2,1,0:T(8,128)(2,1)} %bitcast.13), custom_call_target="tpu_custom_call" | custom-call | flops 4000000000 | bytes 4000000 | tf_op jit(solution)/shard_map/pallas_call | solution.py:236
  41.1 5.4 %collective-permute-start.5 = (bf16[20,32,128]{2,1,0:T(8,128)(2,1)S(1)}, bf16[20,32,128]{2,1,0:T(8,128)(2,1)S(1)}, u32[]{:S(2)}, u32[]{:S(2)}) collective-permute-start(bf16[20,32,128]{2,1,0:T(8,128)(2,1)S(1)} %get-tuple-element.6), channel_id=1, source_target_pairs={{0,16},{8,24},{1,17},{9,25},{2,18},{10,26},{3,19},{11,27},{4,20},{... | collective-permute-start | bytes 491528 | tf_op jit(solution)/shard_map/ppermute | solution.py:20
  46.5 1.5 %collective-permute-start.4 = (bf16[20,32,128]{2,1,0:T(8,128)(2,1)S(1)}, bf16[20,32,128]{2,1,0:T(8,128)(2,1)S(1)}, u32[]{:S(2)}, u32[]{:S(2)}) collective-permute-start(bf16[20,32,128]{2,1,0:T(8,128)(2,1)S(1)} %get-tuple-element.6), channel_id=1, source_target_pairs={{16,0},{24,8},{17,1},{25,9},{18,2},{26,10},{19,3},{27,11},{20,4},{... | collective-permute-start | bytes 491528 | tf_op jit(solution)/shard_map/ppermute | solution.py:20
  48.0 0.0 collective-permute-done.2
  48.0 0.0 collective-permute-done.3
  48.1 5.6 %collective-permute-done.4 = bf16[20,32,128]{2,1,0:T(8,128)(2,1)S(1)} collective-permute-done((bf16[20,32,128]{2,1,0:T(8,128)(2,1)S(1)}, bf16[20,32,128]{2,1,0:T(8,128)(2,1)S(1)}, u32[]{:S(2)}, u32[]{:S(2)}) %collective-permute-start.4) | collective-permute-done | bytes 163872 | tf_op jit(solution)/shard_map/ppermute | solution.py:20
  53.7 0.0 collective-permute-done.5
  53.8 0.0 copy-start.1
  53.8 0.9 %copy-done.1 = bf16[20,160,128]{2,1,0:T(8,128)(2,1)} copy-done((bf16[20,160,128]{2,1,0:T(8,128)(2,1)}, bf16[20,160,128]{2,1,0:T(8,128)(2,1)S(1)}, u32[]{:S(2)}) %copy-start.1) | copy-done | bytes 819224
  54.7 12.8 %shard_map.48 = f32[20,32,128]{2,1,0:T(8,128)} custom-call(s32[1]{0:T(128)} %bitcast.px, s32[1]{0:T(128)} %bitcast.1.py, bf16[20,160,128]{2,1,0:T(8,128)(2,1)} %copy-done.1, bf16[36,20,20]{2,1,0:T(8,128)(2,1)} %bitcast.11, bf16[2,20,20]{2,1,0:T(8,128)(2,1)} %bitcast.12, f32[20,32,128]{2,1,0:T(8,128)} %shard_map.47.fine), custom_call_target="tpu_custom_call" | custom-call | tf_op jit(solution)/shard_map/pallas_call | solution.py:243
  67.5 1.0 %slice.4 = f32[20,20,80]{2,1,0:T(8,128)S(1)} slice(f32[20,32,128]{2,1,0:T(8,128)} %shard_map.48), slice={[0:20], [0:20], [0:80]} | slice | bytes 256000 | tf_op jit(solution)/shard_map/slice | solution.py:251
  68.5 0.4 reshape.30
  68.8 0.1 copy.14
  68.9 1.1 %reshape.31 = f32[1,1,4,8000]{3,2,1,0:T(4,128)} reshape(f32[4,20,20,20]{3,2,1,0:T(8,128)S(1)} %bitcast.9) | data formatting | bytes 256000 | tf_op jit(solution)/shard_map/reshape | solution.py:252
  (8 shorter events, 0.2 us)
Async XLA Ops:
  0.0 1.3 %copy-start.3 = (bf16[1,1,4,8000]{3,2,1,0:T(4,128)(2,1)S(1)}, bf16[1,1,4,8000]{3,2,1,0:T(4,128)(2,1)}, u32[]{:S(2)}) copy-start(bf16[1,1,4,8000]{3,2,1,0:T(4,128)(2,1)} %param.4) | copy-start | bytes 192004
  3.0 2.9 %copy-start.2 = (bf16[20,32,128]{2,1,0:T(8,128)(2,1)S(1)}, bf16[20,32,128]{2,1,0:T(8,128)(2,1)}, u32[]{:S(2)}) copy-start(bf16[20,32,128]{2,1,0:T(8,128)(2,1)} %get-tuple-element.8.u_ref) | copy-start | bytes 491524
  3.0 12.1 %copy-start.4 = (bf16[2,20,20]{2,0,1:T(2,128)(2,1)S(1)}, bf16[2,20,20]{2,0,1:T(2,128)(2,1)}, u32[]{:S(2)}) copy-start(bf16[2,20,20]{2,0,1:T(2,128)(2,1)} %param.7) | copy-start | bytes 4804
  5.4 10.4 %collective-permute-start = (bf16[20,32,128]{2,1,0:T(8,128)(2,1)}, bf16[20,32,128]{2,1,0:T(8,128)(2,1)S(1)}, u32[]{:S(2)}, u32[]{:S(2)}) collective-permute-start(bf16[20,32,128]{2,1,0:T(8,128)(2,1)} %shard_map.46), channel_id=1, source_target_pairs={{0,8},{8,0},{16,24},{24,16},{1,9},{9,1},{17,25},{25,17},{2,10},{10... | collective-permute-start | bytes 491528 | tf_op jit(solution)/shard_map/ppermute | solution.py:25
  5.9 13.4 %collective-permute-start.9 = (bf16[20,32,128]{2,1,0:T(8,128)(2,1)S(1)}, bf16[20,32,128]{2,1,0:T(8,128)(2,1)S(1)}, u32[]{:S(2)}, u32[]{:S(2)}) collective-permute-start(bf16[20,32,128]{2,1,0:T(8,128)(2,1)S(1)} %copy-done.2), channel_id=1, source_target_pairs={{0,1},{1,2},{2,3},{3,4},{4,5},{5,6},{6,7},{8,9},{9,10},{10,11},{11... | collective-permute-start | bytes 491528 | tf_op jit(solution)/shard_map/ppermute | solution.py:20
  10.3 8.9 %collective-permute-start.8 = (bf16[20,32,128]{2,1,0:T(8,128)(2,1)S(1)}, bf16[20,32,128]{2,1,0:T(8,128)(2,1)S(1)}, u32[]{:S(2)}, u32[]{:S(2)}) collective-permute-start(bf16[20,32,128]{2,1,0:T(8,128)(2,1)S(1)} %copy-done.2), channel_id=1, source_target_pairs={{1,0},{2,1},{3,2},{4,3},{5,4},{6,5},{7,6},{9,8},{10,9},{11,10},{12... | collective-permute-start | bytes 491528 | tf_op jit(solution)/shard_map/ppermute | solution.py:20
  11.6 7.6 %collective-permute-start.7 = (bf16[20,32,128]{2,1,0:T(8,128)(2,1)S(1)}, bf16[20,32,128]{2,1,0:T(8,128)(2,1)S(1)}, u32[]{:S(2)}, u32[]{:S(2)}) collective-permute-start(bf16[20,32,128]{2,1,0:T(8,128)(2,1)S(1)} %copy-done.2), channel_id=1, source_target_pairs={{0,8},{8,16},{16,24},{1,9},{9,17},{17,25},{2,10},{10,18},{18,26},{... | collective-permute-start | bytes 491528 | tf_op jit(solution)/shard_map/ppermute | solution.py:20
  13.7 5.4 %collective-permute-start.6 = (bf16[20,32,128]{2,1,0:T(8,128)(2,1)S(1)}, bf16[20,32,128]{2,1,0:T(8,128)(2,1)S(1)}, u32[]{:S(2)}, u32[]{:S(2)}) collective-permute-start(bf16[20,32,128]{2,1,0:T(8,128)(2,1)S(1)} %copy-done.2), channel_id=1, source_target_pairs={{8,0},{16,8},{24,16},{9,1},{17,9},{25,17},{10,2},{18,10},{26,18},{... | collective-permute-start | bytes 491528 | tf_op jit(solution)/shard_map/ppermute | solution.py:20
  16.7 5.9 %collective-permute-start.1 = (bf16[20,32,128]{2,1,0:T(8,128)(2,1)S(1)}, bf16[20,32,128]{2,1,0:T(8,128)(2,1)S(1)}, u32[]{:S(2)}, u32[]{:S(2)}) collective-permute-start(bf16[20,32,128]{2,1,0:T(8,128)(2,1)S(1)} %fusion), channel_id=1, source_target_pairs={{0,1},{1,0},{2,3},{3,2},{4,5},{5,4},{6,7},{7,6},{8,9},{9,8},{10,11... | collective-permute-start | bytes 491528 | tf_op jit(solution)/shard_map/ppermute | solution.py:25
  19.3 3.3 %copy-start = (bf16[20,32,128]{2,1,0:T(8,128)(2,1)S(1)}, bf16[20,32,128]{2,1,0:T(8,128)(2,1)}, u32[]{:S(2)}) copy-start(bf16[20,32,128]{2,1,0:T(8,128)(2,1)} %shard_map.46) | copy-start | bytes 491524
  19.3 9.8 %copy-start.5 = (bf16[20,160,128]{2,1,0:T(8,128)(2,1)}, bf16[20,160,128]{2,1,0:T(8,128)(2,1)S(1)}, u32[]{:S(2)}) copy-start(bf16[20,160,128]{2,1,0:T(8,128)(2,1)S(1)} %constant_dynamic-update-slice_fusion.5.u_ref) | copy-start | bytes 2457604
  22.7 25.3 %collective-permute-start.3 = (bf16[20,32,128]{2,1,0:T(8,128)(2,1)S(1)}, bf16[20,32,128]{2,1,0:T(8,128)(2,1)S(1)}, u32[]{:S(2)}, u32[]{:S(2)}) collective-permute-start(bf16[20,32,128]{2,1,0:T(8,128)(2,1)S(1)} %get-tuple-element.6), channel_id=1, source_target_pairs={{0,2},{1,3},{2,4},{3,5},{4,6},{5,7},{8,10},{9,11},{10,12},{11,13},... | collective-permute-start | bytes 491528 | tf_op jit(solution)/shard_map/ppermute | solution.py:20
  27.9 20.1 %collective-permute-start.2 = (bf16[20,32,128]{2,1,0:T(8,128)(2,1)S(1)}, bf16[20,32,128]{2,1,0:T(8,128)(2,1)S(1)}, u32[]{:S(2)}, u32[]{:S(2)}) collective-permute-start(bf16[20,32,128]{2,1,0:T(8,128)(2,1)S(1)} %get-tuple-element.6), channel_id=1, source_target_pairs={{2,0},{3,1},{4,2},{5,3},{6,4},{7,5},{10,8},{11,9},{12,10},{13,11},... | collective-permute-start | bytes 491528 | tf_op jit(solution)/shard_map/ppermute | solution.py:20
  41.1 12.6 %collective-permute-start.5 = (bf16[20,32,128]{2,1,0:T(8,128)(2,1)S(1)}, bf16[20,32,128]{2,1,0:T(8,128)(2,1)S(1)}, u32[]{:S(2)}, u32[]{:S(2)}) collective-permute-start(bf16[20,32,128]{2,1,0:T(8,128)(2,1)S(1)} %get-tuple-element.6), channel_id=1, source_target_pairs={{0,16},{8,24},{1,17},{9,25},{2,18},{10,26},{3,19},{11,27},{4,20},{... | collective-permute-start | bytes 491528 | tf_op jit(solution)/shard_map/ppermute | solution.py:20
  46.5 7.2 %collective-permute-start.4 = (bf16[20,32,128]{2,1,0:T(8,128)(2,1)S(1)}, bf16[20,32,128]{2,1,0:T(8,128)(2,1)S(1)}, u32[]{:S(2)}, u32[]{:S(2)}) collective-permute-start(bf16[20,32,128]{2,1,0:T(8,128)(2,1)S(1)} %get-tuple-element.6), channel_id=1, source_target_pairs={{16,0},{24,8},{17,1},{25,9},{18,2},{26,10},{19,3},{27,11},{20,4},{... | collective-permute-start | bytes 491528 | tf_op jit(solution)/shard_map/ppermute | solution.py:20
  53.8 0.9 %copy-start.1 = (bf16[20,160,128]{2,1,0:T(8,128)(2,1)}, bf16[20,160,128]{2,1,0:T(8,128)(2,1)S(1)}, u32[]{:S(2)}) copy-start(bf16[20,160,128]{2,1,0:T(8,128)(2,1)S(1)} %constant_dynamic-update-slice_fusion.u_ref) | copy-start | bytes 2457604
